TPU v7x, 256 devices: a whole 4x4x8 slice. The times are simulated.
256 devices in a mesh: width: 8 (over y, core), hidden: 32 (over z, x).
Axes of the slice: x: 4, y: 4, z: 8, core: 2. Of those that a mesh axis runs over, the one named last changes fastest.
Arguments:
- tokens: bfloat16 [1152, 5120], P(None, 'width'), may hold values from -6 to 6
- cotangent: bfloat16 [1152, 5120], P(None, 'width'), may hold values from -6 to 6
- w_up: bfloat16 [5120, 13824], P('width', 'hidden'), may hold values from -0.078125 to 0.078125
- bias_up: float32 [13824], P('hidden'), may hold values from -3 to 3
- w_down: bfloat16 [13824, 5120], P('hidden', 'width'), may hold values from -0.0546875 to 0.0546875
- mod_table: float32 [32, 3, 5120], P(None, None, 'width'), may hold values from -3 to 3
- seg_ids: int32 [1152], replicated, may hold values from 0 to 15, never falling along the last dimension, each value on 1 to 144 neighbouring positions
- step_ids: int32 [16], replicated, may hold values from 0 to 31
Outputs:
- grad_x: bfloat16 [1152, 5120], P(None, 'width')
- grad_up: float32 [5120, 13824], P('width', 'hidden')
- grad_down: float32 [13824, 5120], P('hidden', 'width')
- grad_bias: float32 [13824], P('hidden')
- grad_table: float32 [32, 3, 5120], P(None, None, 'width')
Inputs may be any that keep to these rules, and one draw needn't show every extreme that they name: `seg_ids`: request numbers never fall along the tokens and every request holds at least one token.
All inputs are finite; a program needn't handle non-finite values.
Results may differ from a plain program's by a relative error of at most 0.0063.
Values may be sent and summed in bfloat16 or wider, within the bound.
A program may use at most 64 MiB of HBM per device.

v0:
```python
import jax
import jax.numpy as jnp
from jax import lax
from jax.sharding import PartitionSpec as P

D = 5120


def gelu_tanh(value):
    return jax.nn.gelu(value, approximate=True)


def norm_back(d_norm, x_hat, mod_gain, inv_std, cotangent):
    d_hat = d_norm * mod_gain
    feature_sums = lax.psum((jnp.sum(d_hat, 1), jnp.sum(d_hat * x_hat, 1)), "width")
    mean_one = feature_sums[0] / D
    mean_two = feature_sums[1] / D
    grad_rows = cotangent.astype(jnp.float32) + inv_std[:, None] * (
        d_hat - mean_one[:, None] - x_hat * mean_two[:, None]
    )
    return grad_rows.astype(jnp.bfloat16)


def per_device(tokens, cotangent, w_up, bias_up, w_down, mod_table, seg_ids, step_ids):
    highest = lax.Precision.HIGHEST
    req_count = step_ids.shape[0]
    table_rows = mod_table.shape[0]
    req_of = (seg_ids[:, None] == jnp.arange(req_count)[None, :]).astype(jnp.float32)
    step_of = (step_ids[:, None] == jnp.arange(table_rows)[None, :]).astype(jnp.float32)
    req_mod = jnp.einsum("rk,kcd->rcd", step_of, mod_table, precision=highest)
    shift_tok = jnp.dot(req_of, req_mod[:, 0], precision=highest)
    scale_tok = jnp.dot(req_of, req_mod[:, 1], precision=highest)
    gate_tok = jnp.dot(req_of, req_mod[:, 2], precision=highest)
    x_full = tokens.astype(jnp.float32)
    moment_one, moment_two = lax.psum((jnp.sum(x_full, 1), jnp.sum(x_full * x_full, 1)), "width")
    tok_mean = moment_one / D
    tok_var = moment_two / D - tok_mean * tok_mean
    inv_std = lax.rsqrt(tok_var + 1e-06)
    x_hat = (x_full - tok_mean[:, None]) * inv_std[:, None]
    mod_gain = 1.0 + scale_tok
    normed = (x_hat * mod_gain + shift_tok).astype(jnp.bfloat16)
    up_part = jnp.dot(normed, w_up, preferred_element_type=jnp.float32)
    pre_share = lax.psum(up_part, "width") + bias_up
    hidden_act = gelu_tanh(pre_share).astype(jnp.bfloat16)
    y_part = jnp.dot(hidden_act, w_down, preferred_element_type=jnp.float32)
    gate_part = jnp.dot(req_of.T, cotangent.astype(jnp.float32) * y_part, precision=highest)
    d_out = (cotangent.astype(jnp.float32) * gate_tok).astype(jnp.bfloat16)
    down_part = jnp.dot(d_out, w_down.T, preferred_element_type=jnp.float32)
    act_grad = lax.psum(down_part, "width")
    _, pull = jax.vjp(gelu_tanh, pre_share)
    pre_grad = pull(act_grad)[0]
    grad_bias = jnp.sum(pre_grad, 0)
    d_pre_b = pre_grad.astype(jnp.bfloat16)
    grad_down = jnp.dot(hidden_act.T, d_out, preferred_element_type=jnp.float32)
    grad_up = jnp.dot(normed.T, d_pre_b, preferred_element_type=jnp.float32)
    d_part = jnp.dot(d_pre_b, w_up.T, preferred_element_type=jnp.float32)
    shift_part = jnp.dot(req_of.T, d_part, precision=highest)
    scale_part = jnp.dot(req_of.T, d_part * x_hat, precision=highest)
    req_grads = lax.psum(jnp.stack([shift_part, scale_part, gate_part], 1), "hidden")
    grad_table = jnp.einsum("rk,rcd->kcd", step_of, req_grads, precision=highest)
    d_norm = lax.psum(d_part, "hidden")
    grad_x = norm_back(d_norm, x_hat, mod_gain, inv_std, cotangent)
    return (grad_x, grad_up, grad_down, grad_bias, grad_table)


def solution(mesh):
    placed = (
        P(None, "width"),
        P(None, "width"),
        P("width", "hidden"),
        P("hidden"),
        P("hidden", "width"),
        P(None, None, "width"),
        P(),
        P(),
    )
    return jax.shard_map(
        per_device,
        mesh=mesh,
        in_specs=placed,
        out_specs=(
            P(None, "width"),
            P("width", "hidden"),
            P("hidden", "width"),
            P("hidden"),
            P(None, None, "width"),
        ),
        check_vma=False,
    )
```

profile of v0, /device:TPU:2, one launch (start us, length us, event | category | flops | bytes accessed | tf_op | source)
XLA Modules:
  0.0 338.5 jit_solution(2500453837761555795)
XLA Ops:
  7.2 1.9 fusion.3
  9.2 1.3 fusion.38
  10.5 2.1 convolution_add_fusion.1
  12.7 2.6 fusion
  15.3 25.9 %all-reduce.2 = (f32[1152]{0:T(1024)S(1)}, f32[1152]{0:T(1024)S(1)}) all-reduce(f32[1152]{0:T(1024)S(1)} %get-tuple-element.8, f32[1152]{0:T(1024)S(1)} %get-tuple-element.7), channel_id=1, replica_groups=mesh['width'=8,'hidden'=32] {'width'}, use_global_device_ids=true, to_apply=%region_3.0 | all-reduce | flops 2304 | bytes 18432 | tf_op jit(solution)/shard_map/psum | solution.py:35
  41.2 3.9 %fusion.46 = f32[1152,432]{0,1:T(8,128)} fusion(bf16[1152,640]{1,0:T(8,128)(2,1)} %fusion, bf16[432,640]{1,0:T(8,128)(2,1)S(1)} %copy-done), kind=kOutput, calls=%fused_computation.63 | convolution fusion | flops 637009920 | bytes 4018176 | tf_op jit(solution)/shard_map/dot_general | solution.py:48
  45.0 3.3 fusion.1
  48.4 1.1 copy-done.7
  49.5 2.3 fusion.47
  52.1 77.3 %all-reduce.9.cloned.1.call-done = (f32[1152,432]{0,1:T(8,128)}, f32[1152,432]{0,1:T(8,128)}) async-done(((f32[1152,432]{0,1:T(8,128)}, f32[1152,432]{0,1:T(8,128)}), (f32[1152,432]{0,1:T(8,128)}, f32[1152,432]{0,1:T(8,128)})) %all-reduce.9.cloned.1.call-update) | async-done | bytes 3981328 | tf_op jit(solution)/shard_map/psum | solution.py:49
  129.3 3.2 convert_multiply_fusion.1
  132.6 2.2 fusion.44
  134.8 1.1 fusion.27
  136.2 1.6 fusion.22
  137.8 1.3 convolution_bitcast_fusion.1
  139.1 1.3 convolution_bitcast_fusion
  141.1 0.7 copy-done.8
  141.8 2.0 fusion.25
  143.8 2.5 fusion.42
  146.3 151.9 %all-reduce.7.cloned.1.call-done = (f32[1152,640]{1,0:T(8,128)}, f32[16,3,640]{2,0,1:T(8,128)}) async-done(((f32[1152,640]{1,0:T(8,128)}, f32[16,3,640]{2,0,1:T(8,128)}), (f32[1152,640]{1,0:T(8,128)}, f32[16,3,640]{2,0,1:T(8,128)})) %all-reduce.7.cloned.1.call-update) | async-done | bytes 3072016 | tf_op jit(solution)/shard_map/psum | solution.py:61
  298.2 5.3 %fusion.43 = (f32[1152]{0:T(1024)S(1)}, f32[1152]{0:T(1024)S(1)}, f32[1152,640]{1,0:T(8,128)}) fusion(f32[1152]{0:T(1024)S(1)} %get-tuple-element.21, f32[1152]{0:T(1024)S(1)} %get-tuple-element.20, bf16[1152,640]{1,0:T(8,128)(2,1)S(1)} %copy-done.4, f32[1152,640]{1,0:T(8,128)} %get-tuple-element.9, f32[1152,640]{1,0:T(8,128)} %copy-done.5), kind=kLoop, calls=%fused_computation.61 | loop fusion | flops 5158656 | bytes 10340352 | tf_op jit(solution)/shard_map/reduce_sum | solution.py:15
  303.6 1.1 fusion.36
  304.6 23.6 %all-reduce.1 = (f32[1152]{0:T(1024)S(1)}, f32[1152]{0:T(1024)S(1)}) all-reduce(f32[1152]{0:T(1024)S(1)} %get-tuple-element.6, f32[1152]{0:T(1024)S(1)} %get-tuple-element.5), channel_id=1, replica_groups=mesh['width'=8,'hidden'=32] {'width'}, use_global_device_ids=true, to_apply=%region_10.0 | all-reduce | flops 2304 | bytes 18432 | tf_op jit(solution)/shard_map/psum | solution.py:15
  328.2 3.5 %fusion.2 = bf16[1152,640]{1,0:T(8,128)(2,1)} fusion(bf16[1152,640]{1,0:T(8,128)(2,1)S(1)} %copy-done.11, bf16[1152,640]{1,0:T(8,128)(2,1)S(1)} %copy-done.4, f32[1152,640]{1,0:T(8,128)} %get-tuple-element.19, f32[1152]{0:T(1024)S(1)} %get-tuple-element.22, f32[1152]{0:T(1024)S(1)} %get-tuple-element.23, f32[1152]{0:T(1024)S(1)} %get-tuple-element.20, ...), kind=kLoop, calls=%fused_computation.10 | loop fusion | flops 7372800 | bytes 7391232 | tf_op jit(solution)/shard_map/convert_element_type | solution.py:21
  (49 shorter events, 1.3 us)
Async XLA Ops:
  7.2 34.0 %copy-start = (bf16[432,640]{1,0:T(8,128)(2,1)S(1)}, bf16[432,640]{1,0:T(8,128)(2,1)}, u32[]{:S(2)}) copy-start(bf16[432,640]{1,0:T(8,128)(2,1)} %param.12) | copy-start | bytes 1658884
  7.2 122.1 %all-reduce.9.cloned.1.call-start = ((), (), s32[]{:S(2)}) async-start(), calls=%async_computation.1 | async-start | bytes 7962624 | tf_op jit(solution)/shard_map/psum | solution.py:49
  9.2 3.5 %copy-start.9 = (bf16[1152,640]{1,0:T(8,128)(2,1)S(1)}, bf16[1152,640]{1,0:T(8,128)(2,1)}, u32[]{:S(2)}) copy-start(bf16[1152,640]{1,0:T(8,128)(2,1)} %param.9) | copy-start | bytes 4423684
  9.2 3.5 %copy-start.18 = (s32[1152]{0:T(1024)S(1)}, s32[1152]{0:T(1024)}, u32[]{:S(2)}) copy-start(s32[1152]{0:T(1024)} %param.14) | copy-start | bytes 13828
  10.5 4.8 %copy-start.17 = (f32[16,3,640]{2,0,1:T(8,128)}, f32[16,3,640]{2,0,1:T(8,128)S(1)}, u32[]{:S(2)}) copy-start(f32[16,3,640]{2,0,1:T(8,128)S(1)} %fusion.38) | copy-start | bytes 368644
  12.7 32.4 %copy-start.5 = (f32[1152,640]{1,0:T(8,128)}, f32[1152,640]{1,0:T(8,128)S(1)}, u32[]{:S(2)}) copy-start(f32[1152,640]{1,0:T(8,128)S(1)} %convolution_add_fusion.1) | copy-start | bytes 8847364
  41.2 3.9 %copy-start.2 = (bf16[1152,640]{1,0:T(8,128)(2,1)S(1)}, bf16[1152,640]{1,0:T(8,128)(2,1)}, u32[]{:S(2)}) copy-start(bf16[1152,640]{1,0:T(8,128)(2,1)} %param.8) | copy-start | bytes 4423684
  45.0 4.4 %copy-start.12 = (bf16[640,432]{0,1:T(8,128)(2,1)S(1)}, bf16[640,432]{0,1:T(8,128)(2,1)}, u32[]{:S(2)}) copy-start(bf16[640,432]{0,1:T(8,128)(2,1)} %param.10) | copy-start | bytes 1658884
  48.3 1.1 copy-start.7
  51.8 77.5 %copy-start.10 = (bf16[1152,640]{1,0:T(8,128)(2,1)S(1)}, bf16[1152,640]{1,0:T(8,128)(2,1)}, u32[]{:S(2)}) copy-start(bf16[1152,640]{1,0:T(8,128)(2,1)} %param.9) | copy-start | bytes 4423684
  51.8 77.5 %copy-start.20 = (f32[432]{0:T(512)S(1)}, f32[432]{0:T(512)}, u32[]{:S(2)}) copy-start(f32[432]{0:T(512)} %param.11) | copy-start | bytes 5188
  51.8 246.4 %all-reduce.7.cloned.1.call-start = ((), (), s32[]{:S(2)}) async-start(), calls=%async_computation | async-start | bytes 6144000 | tf_op jit(solution)/shard_map/psum | solution.py:61
  129.3 3.2 copy-start.14
  129.3 3.2 copy-start.16
  132.6 2.2 copy-start.13
  134.8 1.4 copy-start.3
  136.2 1.6 copy-start.1
  140.4 1.4 copy-start.8
  141.8 2.0 copy-start.6
  141.8 2.0 copy-start.15
  143.8 154.4 %copy-start.4 = (bf16[1152,640]{1,0:T(8,128)(2,1)S(1)}, bf16[1152,640]{1,0:T(8,128)(2,1)}, u32[]{:S(2)}) copy-start(bf16[1152,640]{1,0:T(8,128)(2,1)} %param.8) | copy-start | bytes 4423684
  298.2 5.3 %copy-start.19 = (f32[16,3,640]{2,0,1:T(8,128)S(1)}, f32[16,3,640]{2,0,1:T(8,128)}, u32[]{:S(2)}) copy-start(f32[16,3,640]{2,0,1:T(8,128)} %get-tuple-element.10) | copy-start | bytes 368644
  298.2 5.3 %copy-start.21 = (s32[16]{0:T(128)S(1)}, s32[16]{0:T(128)}, u32[]{:S(2)}) copy-start(s32[16]{0:T(128)} %param.15) | copy-start | bytes 196
  298.2 30.0 %copy-start.11 = (bf16[1152,640]{1,0:T(8,128)(2,1)S(1)}, bf16[1152,640]{1,0:T(8,128)(2,1)}, u32[]{:S(2)}) copy-start(bf16[1152,640]{1,0:T(8,128)(2,1)} %param.9) | copy-start | bytes 4423684
Sparse Core Ops, SparseCore 0:
  51.9 77.3 all-reduce.8
  141.2 157.0 all-reduce.6
where the time goes:
time: 339 us
  waiting for transfers between devices  229 us (68%)
  blocking collectives  49.4 us (15%)
  matrix products  29.6 us (9%)
  between operations  14.2 us (4%)
  other arithmetic  13.7 us (4%)
    psum x1, waiting for transfers between devices, per_device(): d_norm = lax.psum(d_part, 'hidden')  152 us
    psum x1, waiting for transfers between devices, per_device(): act_grad = lax.psum(down_part, 'width')  77.3 us
    psum x1, blocking collectives, per_device(): lax.psum((jnp.sum(x_full, 1), jnp.sum(x_full * x_full, 1)), 'width')  25.9 us
    psum x1, blocking collectives, norm_back(): lax.psum((jnp.sum(d_hat, 1), jnp.sum(d_hat * x_hat, 1)), 'width')  23.6 us
  transfers between devices with their start and end apart: 2, of which 2 were waited for; matrix products, arithmetic and copies ran while one was open for 1% of the time, Pallas kernels for 0%

commit v1 on v0

--- a/solution.py
+++ b/solution.py
@@ -46,7 +46,11 @@
     gate_part = jnp.dot(req_of.T, cotangent.astype(jnp.float32) * y_part, precision=highest)
     d_out = (cotangent.astype(jnp.float32) * gate_tok).astype(jnp.bfloat16)
     down_part = jnp.dot(d_out, w_down.T, preferred_element_type=jnp.float32)
-    act_grad = lax.psum(down_part, "width")
+    act_grad = down_part
+    for hop in (1, 2, 4):
+        act_grad = act_grad + lax.ppermute(
+            act_grad, "width", [(dev, dev ^ hop) for dev in range(8)]
+        )
     _, pull = jax.vjp(gelu_tanh, pre_share)
     pre_grad = pull(act_grad)[0]
     grad_bias = jnp.sum(pre_grad, 0)

time: 339 us -> 396 us (1.17)
  blocking collectives: 49.4 us -> 85.1 us
  waiting for transfers between devices: 229 us -> 245 us
  other arithmetic: 13.7 us -> 20.3 us
    psum x1, blocking collectives: 25.9 us -> 61.5 us  [per_device(): lax.psum((jnp.sum(x_full, 1), jnp.sum(x_full * x_full, 1)), 'width')]
    psum x1, waiting for transfers between devices: 77.3 us -> 90.5 us  [per_device(): pre_share = lax.psum(up_part, 'width') + bias_up]
    add x0 -> x2, other arithmetic: none -> 5.82 us  [per_device(): act_grad + lax.ppermute(act_grad, 'width', [(dev, dev ^ hop) for dev in r...]
    ppermute x0 -> x3, waiting for transfers between devices: none -> 4 us  [per_device(): lax.ppermute(act_grad, 'width', [(dev, dev ^ hop) for dev in range(8)])]
  transfers between devices with their start and end apart: 2 -> 5, of which waited for: 2 -> 3; matrix products, arithmetic and copies ran while one was open for 1% -> 5% of each run, Pallas kernels for 0% -> 0%
where the time goes in v1:
time: 396 us
  waiting for transfers between devices  245 us (62%)
  blocking collectives  85.1 us (21%)
  matrix products  28.6 us (7%)
  other arithmetic  20.3 us (5%)
  between operations  14.3 us (4%)
    psum x1, waiting for transfers between devices, per_device(): d_norm = lax.psum(d_part, 'hidden')  150 us
    psum x1, waiting for transfers between devices, per_device(): pre_share = lax.psum(up_part, 'width') + bias_up  90.5 us
    psum x1, blocking collectives, per_device(): lax.psum((jnp.sum(x_full, 1), jnp.sum(x_full * x_full, 1)), 'width')  61.5 us
    psum x1, blocking collectives, norm_back(): lax.psum((jnp.sum(d_hat, 1), jnp.sum(d_hat * x_hat, 1)), 'width')  23.6 us
  transfers between devices with their start and end apart: 5, of which 3 were waited for; matrix products, arithmetic and copies ran while one was open for 5% of the time, Pallas kernels for 0%

profile of v1, /device:TPU:2, one launch (start us, length us, event | category | flops | bytes accessed | tf_op | source)
XLA Modules:
  0.0 395.9 jit_solution(8436769385280361114)
XLA Ops:
  7.2 1.3 fusion.38
  8.5 2.8 fusion
  12.6 4.0 %collective-permute-done = f32[1152,432]{0,1:T(8,128)S(1)} collective-permute-done((f32[1152,432]{0,1:T(8,128)S(1)}, f32[1152,432]{0,1:T(8,128)S(1)}, u32[]{:S(2)}, u32[]{:S(2)}) %collective-permute-start) | collective-permute-done | bytes 1990688 | tf_op jit(solution)/shard_map/ppermute | solution.py:51
  16.6 1.6 add.60
  18.2 1.6 collective-permute-start.1
  20.3 61.5 %all-reduce.2 = (f32[1152]{0:T(1024)S(1)}, f32[1152]{0:T(1024)S(1)}) all-reduce(f32[1152]{0:T(1024)S(1)} %get-tuple-element.8, f32[1152]{0:T(1024)S(1)} %get-tuple-element.7), channel_id=1, replica_groups=mesh['width'=8,'hidden'=32] {'width'}, use_global_device_ids=true, to_apply=%region_3.0 | all-reduce | flops 2304 | bytes 18432 | tf_op jit(solution)/shard_map/psum | solution.py:35
  81.8 2.2 convolution_add_fusion.1
  84.0 3.3 fusion.1
  87.3 4.2 %add.61 = f32[1152,432]{0,1:T(8,128)} add(f32[1152,432]{0,1:T(8,128)} %add.60, f32[1152,432]{0,1:T(8,128)} %collective-permute-done.1) | non-fusion elementwise | flops 497664 | bytes 5971968 | tf_op jit(solution)/shard_map/add | solution.py:51
  91.5 2.4 fusion.47
  94.2 90.5 %all-reduce.6.cloned.1.call-done = f32[1152,432]{0,1:T(8,128)} async-done(((f32[1152,432]{0,1:T(8,128)}), f32[1152,432]{0,1:T(8,128)}) %all-reduce.6.cloned.1.call-update) | async-done | bytes 1990672 | tf_op jit(solution)/shard_map/psum | solution.py:43
  184.7 3.1 convert_multiply_fusion.1
  187.8 1.3 convolution_bitcast_fusion
  189.3 4.4 %fusion.44 = (f32[432]{0:T(512)}, bf16[1152,432]{0,1:T(8,128)(2,1)S(1)}) fusion(f32[1152,432]{0,1:T(8,128)S(1)} %copy-done.14, f32[432]{0:T(512)S(1)} %copy-done.18, f32[1152,432]{0,1:T(8,128)} %add.61, f32[1152,432]{0,1:T(8,128)} %collective-permute-done.2), kind=kLoop, calls=%fused_computation.62 | loop fusion | flops 11445840 | bytes 6970752 | tf_op jit(solution)/shard_map/reduce_sum | solution.py:56
  193.7 1.1 fusion.27
  195.5 1.6 fusion.22
  197.1 1.3 convolution_bitcast_fusion.1
  199.1 4.2 %fusion.42 = f32[432,640]{1,0:T(8,128)} fusion(bf16[1152,640]{1,0:T(8,128)(2,1)S(1)} %fusion, f32[1152,432]{0,1:T(8,128)} %all-reduce.6.cloned.1.call-done, f32[432]{0:T(512)S(1)} %copy-done.18), kind=kOutput, calls=%fused_computation.60 | convolution fusion | flops 641986560 | bytes 4572864 | tf_op jit(solution)/shard_map/dot_general | solution.py:58
  203.3 2.0 fusion.25
  205.3 150.2 %all-reduce.8.cloned.1.call-done = (f32[1152,640]{1,0:T(8,128)}, f32[16,3,640]{2,0,1:T(8,128)}) async-done(((f32[1152,640]{1,0:T(8,128)}, f32[16,3,640]{2,0,1:T(8,128)}), (f32[1152,640]{1,0:T(8,128)}, f32[16,3,640]{2,0,1:T(8,128)})) %all-reduce.8.cloned.1.call-update) | async-done | bytes 3072016 | tf_op jit(solution)/shard_map/psum | solution.py:65
  355.5 5.3 %fusion.43 = (f32[1152]{0:T(1024)S(1)}, f32[1152]{0:T(1024)S(1)}, f32[1152,640]{1,0:T(8,128)}) fusion(f32[1152]{0:T(1024)S(1)} %get-tuple-element.19, f32[1152]{0:T(1024)S(1)} %get-tuple-element.18, bf16[1152,640]{1,0:T(8,128)(2,1)S(1)} %copy-done.4, f32[1152,640]{1,0:T(8,128)} %get-tuple-element.9, f32[1152,640]{1,0:T(8,128)} %copy-done.5), kind=kLoop, calls=%fused_computation.61 | loop fusion | flops 5158656 | bytes 10340352 | tf_op jit(solution)/shard_map/reduce_sum | solution.py:15
  360.9 1.1 fusion.36
  362.0 23.6 %all-reduce.1 = (f32[1152]{0:T(1024)S(1)}, f32[1152]{0:T(1024)S(1)}) all-reduce(f32[1152]{0:T(1024)S(1)} %get-tuple-element.6, f32[1152]{0:T(1024)S(1)} %get-tuple-element.5), channel_id=1, replica_groups=mesh['width'=8,'hidden'=32] {'width'}, use_global_device_ids=true, to_apply=%region_9.0 | all-reduce | flops 2304 | bytes 18432 | tf_op jit(solution)/shard_map/psum | solution.py:15
  385.5 3.5 fusion.2
  (53 shorter events, 3.7 us)
Async XLA Ops:
  7.2 4.2 %copy-start = (bf16[432,640]{1,0:T(8,128)(2,1)S(1)}, bf16[432,640]{1,0:T(8,128)(2,1)}, u32[]{:S(2)}) copy-start(bf16[432,640]{1,0:T(8,128)(2,1)} %param.12) | copy-start | bytes 1658884
  7.2 177.5 %all-reduce.6.cloned.1.call-start = ((), (), s32[]{:S(2)}) async-start(), calls=%async_computation | async-start | bytes 3981312 | tf_op jit(solution)/shard_map/psum | solution.py:43
  8.5 4.0 copy-start.15
  12.5 7.3 %copy-start.2 = (bf16[1152,640]{1,0:T(8,128)(2,1)S(1)}, bf16[1152,640]{1,0:T(8,128)(2,1)}, u32[]{:S(2)}) copy-start(bf16[1152,640]{1,0:T(8,128)(2,1)} %param.8) | copy-start | bytes 4423684
  12.5 69.3 %copy-start.16 = (s32[1152]{0:T(1024)S(1)}, s32[1152]{0:T(1024)}, u32[]{:S(2)}) copy-start(s32[1152]{0:T(1024)} %param.14) | copy-start | bytes 13828
  12.5 4.1 %collective-permute-start = (f32[1152,432]{0,1:T(8,128)S(1)}, f32[1152,432]{0,1:T(8,128)S(1)}, u32[]{:S(2)}, u32[]{:S(2)}) collective-permute-start(f32[1152,432]{0,1:T(8,128)S(1)} %fusion.46), channel_id=1, source_target_pairs={{0,32},{32,0},{64,96},{96,64},{128,160},{160,128},{192,224},{224,1... | collective-permute-start | bytes 5971976 | tf_op jit(solution)/shard_map/ppermute | solution.py:51
  18.2 69.1 %collective-permute-start.1 = (f32[1152,432]{0,1:T(8,128)}, f32[1152,432]{0,1:T(8,128)}, u32[]{:S(2)}, u32[]{:S(2)}) collective-permute-start(f32[1152,432]{0,1:T(8,128)} %add.60), channel_id=1, source_target_pairs={{0,64},{32,96},{64,0},{96,32},{128,192},{160,224},{192,128},{224,1... | collective-permute-start | bytes 5971976 | tf_op jit(solution)/shard_map/ppermute | solution.py:51
  84.0 3.3 copy-start.5
  87.3 4.3 %copy-start.6 = (bf16[1152,640]{1,0:T(8,128)(2,1)}, bf16[1152,640]{1,0:T(8,128)(2,1)S(1)}, u32[]{:S(2)}) copy-start(bf16[1152,640]{1,0:T(8,128)(2,1)S(1)} %fusion.1) | copy-start | bytes 4423684
  87.3 4.3 %copy-start.12 = (bf16[640,432]{0,1:T(8,128)(2,1)S(1)}, bf16[640,432]{0,1:T(8,128)(2,1)}, u32[]{:S(2)}) copy-start(bf16[640,432]{0,1:T(8,128)(2,1)} %param.10) | copy-start | bytes 1658884
  91.5 97.5 %collective-permute-start.2 = (f32[1152,432]{0,1:T(8,128)}, f32[1152,432]{0,1:T(8,128)}, u32[]{:S(2)}, u32[]{:S(2)}) collective-permute-start(f32[1152,432]{0,1:T(8,128)} %add.61), channel_id=1, source_target_pairs={{0,128},{32,160},{64,192},{96,224},{128,0},{160,32},{192,64},{224,... | collective-permute-start | bytes 5971976 | tf_op jit(solution)/shard_map/ppermute | solution.py:51
  93.9 90.8 %copy-start.10 = (bf16[1152,640]{1,0:T(8,128)(2,1)S(1)}, bf16[1152,640]{1,0:T(8,128)(2,1)}, u32[]{:S(2)}) copy-start(bf16[1152,640]{1,0:T(8,128)(2,1)} %param.9) | copy-start | bytes 4423684
  93.9 90.8 %copy-start.18 = (f32[432]{0:T(512)S(1)}, f32[432]{0:T(512)}, u32[]{:S(2)}) copy-start(f32[432]{0:T(512)} %param.11) | copy-start | bytes 5188
  93.9 261.6 %all-reduce.8.cloned.1.call-start = ((), (), s32[]{:S(2)}) async-start(), calls=%async_computation.1 | async-start | bytes 6144000 | tf_op jit(solution)/shard_map/psum | solution.py:65
  187.7 1.6 copy-start.14
  189.0 4.7 %copy-start.13 = (bf16[640,432]{0,1:T(8,128)(2,1)S(1)}, bf16[640,432]{0,1:T(8,128)(2,1)}, u32[]{:S(2)}) copy-start(bf16[640,432]{0,1:T(8,128)(2,1)} %param.10) | copy-start | bytes 1658884
  193.7 1.7 copy-start.3
  195.5 1.7 copy-start.1
  199.1 4.2 %copy-start.7 = (bf16[1152,640]{1,0:T(8,128)(2,1)S(1)}, bf16[1152,640]{1,0:T(8,128)(2,1)}, u32[]{:S(2)}) copy-start(bf16[1152,640]{1,0:T(8,128)(2,1)} %copy-done.6) | copy-start | bytes 4423684
  199.1 4.2 %copy-start.9 = (bf16[1152,432]{0,1:T(8,128)(2,1)S(1)}, bf16[1152,432]{0,1:T(8,128)(2,1)}, u32[]{:S(2)}) copy-start(bf16[1152,432]{0,1:T(8,128)(2,1)} %copy-done.8) | copy-start | bytes 2985988
  203.3 152.2 %copy-start.4 = (bf16[1152,640]{1,0:T(8,128)(2,1)S(1)}, bf16[1152,640]{1,0:T(8,128)(2,1)}, u32[]{:S(2)}) copy-start(bf16[1152,640]{1,0:T(8,128)(2,1)} %param.8) | copy-start | bytes 4423684
  355.5 5.4 %copy-start.17 = (f32[16,3,640]{2,0,1:T(8,128)S(1)}, f32[16,3,640]{2,0,1:T(8,128)}, u32[]{:S(2)}) copy-start(f32[16,3,640]{2,0,1:T(8,128)} %get-tuple-element.10) | copy-start | bytes 368644
  355.5 5.4 %copy-start.19 = (s32[16]{0:T(128)S(1)}, s32[16]{0:T(128)}, u32[]{:S(2)}) copy-start(s32[16]{0:T(128)} %param.15) | copy-start | bytes 196
  355.5 30.0 %copy-start.11 = (bf16[1152,640]{1,0:T(8,128)(2,1)S(1)}, bf16[1152,640]{1,0:T(8,128)(2,1)}, u32[]{:S(2)}) copy-start(bf16[1152,640]{1,0:T(8,128)(2,1)} %param.9) | copy-start | bytes 4423684
  (1 other events, 1.1 us)
Sparse Core Ops, SparseCore 0:
  94.1 90.5 all-reduce.5
  199.2 156.2 all-reduce.7
